TPU v7x, 256 devices: a whole 4x4x8 slice. The times are simulated.
256 devices in a mesh: occ: 8 (over x_lo, y), vir: 32 (over z, x_hi, core).
Axes of the slice: x: 4 (x_hi: 2, x_lo: 2; x = x_hi * 2 + x_lo), y: 4, z: 8, core: 2. Of those that a mesh axis runs over, the one named last changes fastest.
Arguments:
- amplitudes: bfloat16 [8192, 65536], P('occ', 'vir'), may hold values from -6 to 6
- integrals: bfloat16 [65536, 2048], P('vir', 'occ'), may hold values from -0.125 to 0.125
- ij_irrep: int32 [8192], P('occ'), may hold values from 0 to 7
- cd_irrep: int32 [65536], P('vir'), may hold values from 0 to 7
Outputs:
- ladder: float32 [8192, 2048], P('occ', 'vir')
All inputs are finite; a program needn't handle non-finite values.
Results may differ from a plain program's by a relative error of at most 0.0003.
Values may be sent and summed in bfloat16 or wider, within the bound.
A program may use at most 64 MiB of HBM per device.

v0:
```python
import jax
import jax.numpy as jnp
from jax import lax
from jax.sharding import PartitionSpec as P


def body(amplitudes, integrals, ij_irrep, cd_irrep):
    masked = jnp.where(
        ij_irrep[:, None] == cd_irrep[None, :], amplitudes, jnp.zeros_like(amplitudes)
    )
    partial_sums = jnp.dot(
        masked,
        lax.all_gather(integrals, "occ", axis=1, tiled=True),
        preferred_element_type=jnp.float32,
    )
    ladder = lax.psum_scatter(partial_sums, "vir", scatter_dimension=1, tiled=True)
    return ladder


def solution(mesh):
    in_specs = (P("occ", "vir"), P("vir", "occ"), P("occ"), P("vir"))
    out_specs = P("occ", "vir")
    return jax.shard_map(body, mesh=mesh, in_specs=in_specs, out_specs=out_specs, check_vma=False)
```

profile of v0, /device:TPU:26, one launch (start us, length us, event | category | flops | bytes accessed | tf_op | source)
XLA Modules:
  0.0 288.6 jit_solution(13729806193446623198)
XLA Ops:
  6.5 0.0 all-gather.2.cloned.1.call-start
  6.5 0.7 all-gather.2.cloned.1.call-update
  7.3 0.0 reduce-scatter.2.cloned.1.call-start
  7.3 104.6 %all-gather.2.cloned.1.call-done = bf16[2048,2048]{1,0:T(8,128)(2,1)} async-done(((bf16[2048,256]{1,0:T(8,128)(2,1)}), bf16[2048,2048]{1,0:T(8,128)(2,1)}) %all-gather.2.cloned.1.call-update) | async-done | bytes 8388624 | tf_op jit(solution)/shard_map/all_gather | solution.py:13
  112.0 14.8 %fusion = f32[1024,2048]{0,1:T(8,128)} fusion(bf16[2048,2048]{1,0:T(8,128)(2,1)} %all-gather.2.cloned.1.call-done, bf16[1024,2048]{1,0:T(8,128)(2,1)} %param.4, s32[2048]{0:T(1024)} %param.7, s32[1024]{0:T(1024)} %param.6), kind=kOutput, calls=%fused_computation.1 | convolution fusion | flops 8594128896 | bytes 20983808 | tf_op jit(solution)/shard_map/dot_general | solution.py:11
  126.7 0.0 reduce-scatter.2.cloned.1.call-update
  126.8 155.0 %reduce-scatter.2.cloned.1.call-done = f32[1024,64]{0,1:T(8,128)} async-done(((f32[1024,2048]{0,1:T(8,128)}), f32[1024,64]{0,1:T(8,128)}) %reduce-scatter.2.cloned.1.call-update) | async-done | bytes 262160 | tf_op jit(solution)/shard_map/reduce_scatter | solution.py:16
Async XLA Ops:
  6.5 105.4 %all-gather.2.cloned.1.call-start = ((), (), s32[]{:S(2)}) async-start(), calls=%async_computation.1 | async-start | bytes 9437184 | tf_op jit(solution)/shard_map/all_gather | solution.py:13
  7.3 274.5 %reduce-scatter.2.cloned.1.call-start = ((), (), s32[]{:S(2)}) async-start(), calls=%async_computation.2 | async-start | bytes 8650752 | tf_op jit(solution)/shard_map/reduce_scatter | solution.py:16
Sparse Core Ops, SparseCore 0:
  9.1 102.8 all-gather.1
  126.9 154.8 reduce-scatter.1
where the time goes:
time: 290 us; the launch traced here: 289 us
  waiting for transfers between devices  260 us (90%)
  matrix products  14.8 us (5%)
  between operations  13.4 us (5%)
    reduce_scatter x1, waiting for transfers between devices, body(): lax.psum_scatter(partial_sums, 'vir', scatter_dimension=1, tiled=True)  155 us
    all_gather x1, waiting for transfers between devices, body(): lax.all_gather(integrals, 'occ', axis=1, tiled=True)  105 us
    dot_general x1, matrix products, body(): jnp.dot(masked, lax.all_gather(integrals, 'occ', axis=1, tiled=True), pre...  14.8 us
  transfers between devices with their start and end apart: 2, of which 2 were waited for; matrix products, arithmetic and copies ran while one was open for 0% of the time, Pallas kernels for 0%

commit v1 on v0

v1 whole, which is shorter than its diff:
```python
import functools

import jax
import jax.numpy as jnp
from jax import lax
from jax.experimental import pallas as pl
from jax.experimental.pallas import tpu as pltpu
from jax.sharding import PartitionSpec as P

MESH = pl.DeviceIdType.MESH

SLOT = {(0, 0): 0, (0, 3): 1, (0, 1): 2, (1, 0): 3, (0, 2): 4, (1, 3): 5, (1, 1): 6, (1, 2): 7}
WHERE = {slot: place for place, slot in SLOT.items()}

EVENTS = (
    (0, 0), (0, 1), (0, 2), (0, 3),
    (1, 0), (2, 1), (3, 0),
    (1, 2), (2, 3), (3, 1),
    (1, 1), (2, 0), (3, 2),
    (1, 3), (2, 2), (3, 3),
    (4, 2), (4, 3), (5, 2),
    (5, 0), (6, 1), (6, 3),
    (5, 3), (4, 0), (4, 1),
    (5, 1), (6, 0), (6, 2),
    (7, 0), (7, 1), (7, 2),
    (7, 3),
)
FORWARDS = {
    9: (
        ("up", 1, 2), ("down", 2, 3), ("across", 1, 2),
        ("up", 3, 0), ("down", 3, 1), ("across", 2, 3),
        ("up", 1, 0), ("down", 2, 1),
        ("up", 3, 1), ("down", 3, 0),
    ),
    15: (("across", 1, 3), ("across", 2, 2)),
    17: (("across", 4, 2), ("across", 4, 3)),
    20: (("up", 5, 0), ("down", 6, 1)),
}
FIRST = (
    ("up", 0, 0), ("down", 0, 1), ("across", 0, 0),
    ("up", 0, 2), ("down", 0, 3), ("across", 0, 1),
    ("up", 0, 1), ("down", 0, 0), ("across", 0, 2),
    ("up", 0, 3), ("down", 0, 2), ("across", 0, 3),
)
SENDS = FIRST + tuple(send for event in sorted(FORWARDS) for send in FORWARDS[event])
LAG = 2
TOP = 32767.0


def landing(way, slot):
    other, step = WHERE[slot]
    if way == "up":
        return SLOT[(other, (step - 1) % 4)]
    if way == "down":
        return SLOT[(other, (step + 1) % 4)]
    return SLOT[(1 - other, step)]


def pick(index, values):
    out = jnp.int32(values[-1])
    for at in range(len(values) - 2, -1, -1):
        out = jnp.where(index == at, jnp.int32(values[at]), out)
    return out


def kernel(
    amp_hbm, int_hbm, ij_ref, cd_ref, out_ref,
    amp, blocks, acc, turned, twin, coded, scale, coded_in, scale_in, total, far, ij_col,
    amp_sem, own_sem, send_sem, recv_sem, twin_send, twin_recv,
    z_send, z_recv, s_send, s_recv, far_send, far_recv,
):
    occ, vir = lax.axis_index("occ"), lax.axis_index("vir")
    x_lo, y = occ // 4, occ % 4
    z, x_hi, core = vir // 4, (vir // 2) % 2, vir % 2
    depth = int_hbm.shape[0] // 4

    amp_in = pltpu.make_async_copy(amp_hbm, amp, amp_sem)
    own_in = pltpu.make_async_copy(int_hbm, blocks.at[0], own_sem)
    amp_in.start()
    own_in.start()

    to = {
        "up": (x_lo * 4 + (y + 1) % 4, vir),
        "down": (x_lo * 4 + (y + 3) % 4, vir),
        "across": ((1 - x_lo) * 4 + y, vir),
    }
    sibling = (occ, vir + 1 - 2 * core)
    beyond = (occ, vir + 2 - 4 * x_hi)

    barrier = pltpu.get_barrier_semaphore()
    for device in (to["up"], to["down"], to["across"], sibling, beyond):
        pl.semaphore_signal(barrier, inc=1, device_id=device, device_id_type=MESH)
    for ahead in range(1, 8):
        pl.semaphore_signal(barrier, inc=1, device_id=(occ, (vir + 4 * ahead) % 32), device_id_type=MESH)
    pl.semaphore_wait(barrier, 12)

    def piece(index):
        way, slot, quarter = SENDS[index]
        rows = pl.ds(quarter * depth, depth)
        return pltpu.make_async_remote_copy(
            src_ref=int_hbm.at[rows, :] if slot == 0 else blocks.at[slot, rows, :],
            dst_ref=blocks.at[landing(way, slot), rows, :],
            send_sem=send_sem.at[index],
            recv_sem=recv_sem.at[landing(way, slot), quarter],
            device_id=to[way],
            device_id_type=MESH,
        )

    for index in range(len(FIRST)):
        piece(index).start()

    acc[...] = jnp.zeros_like(acc)
    ij_col[...] = jnp.broadcast_to(ij_ref[...].astype(jnp.float32), (128, ij_ref.shape[1])).T.astype(jnp.bfloat16)
    cd_row = cd_ref[...].astype(jnp.float32).astype(jnp.bfloat16)
    amp_in.wait()
    for at in range(0, amp.shape[1], 128):
        tile = amp[:, at:at + 128]
        amp[:, at:at + 128] = jnp.where(ij_col[...] == cd_row[:, at:at + 128], tile, jnp.zeros_like(tile))
    own_in.wait()

    def owner(slot):
        other = pick(slot, [WHERE[at][0] for at in range(8)])
        step = pick(slot, [WHERE[at][1] for at in range(8)])
        return ((x_lo + other) % 2) * 4 + (y + step) % 4

    def twin_copy(slot):
        return pltpu.make_async_remote_copy(
            src_ref=turned.at[slot, 1 - core],
            dst_ref=twin.at[slot],
            send_sem=twin_send.at[slot],
            recv_sem=twin_recv.at[slot],
            device_id=sibling,
            device_id_type=MESH,
        )

    def z_copies(slot):
        target = owner(slot)
        place = (z - target + 8) % 8
        device = (occ, target * 4 + x_hi * 2 + core)
        return (
            pltpu.make_async_remote_copy(
                src_ref=coded.at[slot], dst_ref=coded_in.at[place],
                send_sem=z_send.at[slot], recv_sem=z_recv.at[place],
                device_id=device, device_id_type=MESH,
            ),
            pltpu.make_async_remote_copy(
                src_ref=scale.at[slot], dst_ref=scale_in.at[place],
                send_sem=s_send.at[slot], recv_sem=s_recv.at[place],
                device_id=device, device_id_type=MESH,
            ),
        )

    last_of = {}
    for event, (slot, _) in enumerate(EVENTS):
        last_of[slot] = event
    ends = [int(last_of[slot] == event) for event, (slot, _) in enumerate(EVENTS)]
    slots = [slot for slot, _ in EVENTS]
    quarters = [quarter for _, quarter in EVENTS]

    @pl.loop(0, len(EVENTS) + LAG)
    def _(event):
        @pl.when(event < len(EVENTS))
        def _():
            slot, quarter = pick(event, slots), pick(event, quarters)
            rows = pl.ds(pl.multiple_of(quarter * depth, depth), depth)

            @pl.when(slot > 0)
            def _():
                pltpu.make_async_remote_copy(
                    src_ref=blocks.at[slot, rows, :], dst_ref=blocks.at[slot, rows, :],
                    send_sem=send_sem.at[0], recv_sem=recv_sem.at[slot, quarter],
                    device_id=to["up"], device_id_type=MESH,
                ).wait_recv()

            index = len(FIRST)
            for after in sorted(FORWARDS):
                @pl.when(event == after)
                def _(index=index, count=len(FORWARDS[after])):
                    for at in range(count):
                        piece(index + at).start()
                index += len(FORWARDS[after])

            acc[slot] += jnp.dot(amp[:, rows], blocks[slot, rows, :], preferred_element_type=jnp.float32)

            @pl.when(pick(event, ends) == 1)
            def _():
                block = acc[slot].T
                for half in range(2):
                    turned[slot, half, 0:64, :] = block[64 * half:64 * half + 64]
                    turned[slot, half, 64:128, :] = block[128 + 64 * half:192 + 64 * half]
                twin_copy(slot).start()

        earlier = jnp.maximum(event - LAG, 0)

        @pl.when((event >= LAG) & (pick(earlier, ends) == 1))
        def _():
            slot = pick(earlier, slots)
            twin_copy(slot).wait_recv()
            both = turned[slot, core] + twin[slot]
            here = owner(slot) == z

            @pl.when(here)
            def _():
                total[...] = both

            @pl.when(jnp.logical_not(here))
            def _():
                most = jnp.maximum(jnp.max(jnp.abs(both), axis=0, keepdims=True), 1e-30)
                scale[slot] = most * (1.0 / TOP)
                coded[slot] = jnp.round(both * (TOP / most)).astype(jnp.int32).astype(jnp.int16)
                for copy in z_copies(slot):
                    copy.start()

    @pl.loop(1, 8)
    def _(place):
        pltpu.make_async_copy(coded_in.at[place], coded_in.at[place], z_recv.at[place]).wait()
        pltpu.make_async_copy(scale_in.at[place], scale_in.at[place], s_recv.at[place]).wait()
        total[...] += coded_in[place].astype(jnp.int32).astype(jnp.float32) * scale_in[place]

    away = pltpu.make_async_remote_copy(
        src_ref=total.at[pl.ds(pl.multiple_of(64 * (1 - x_hi), 64), 64), :],
        dst_ref=far,
        send_sem=far_send, recv_sem=far_recv,
        device_id=beyond, device_id_type=MESH,
    )
    away.start()
    away.wait_recv()
    out_ref[...] = total[pl.ds(pl.multiple_of(64 * x_hi, 64), 64), :] + far[...]

    away.wait_send()
    for index in range(len(SENDS)):
        piece(index).wait_send()

    @pl.loop(0, 8)
    def _(slot):
        twin_copy(slot).wait_send()

        @pl.when(owner(slot) != z)
        def _():
            for copy in z_copies(slot):
                copy.wait_send()


def body(amplitudes, integrals, ij_irrep, cd_irrep):
    rows, deep = amplitudes.shape
    wide = integrals.shape[1]
    any_space = pl.BlockSpec(memory_space=pl.ANY)
    vmem = pl.BlockSpec(memory_space=pltpu.VMEM)
    dma = pltpu.SemaphoreType.DMA
    out = pl.pallas_call(
        kernel,
        out_shape=jax.ShapeDtypeStruct((64, rows), jnp.float32),
        in_specs=[any_space, any_space, vmem, vmem],
        out_specs=vmem,
        scratch_shapes=[
            pltpu.VMEM((rows, deep), jnp.bfloat16),
            pltpu.VMEM((8, deep, wide), jnp.bfloat16),
            pltpu.VMEM((8, rows, wide), jnp.float32),
            pltpu.VMEM((8, 2, 128, rows), jnp.float32),
            pltpu.VMEM((8, 128, rows), jnp.float32),
            pltpu.VMEM((8, 128, rows), jnp.int16),
            pltpu.VMEM((8, 1, rows), jnp.float32),
            pltpu.VMEM((8, 128, rows), jnp.int16),
            pltpu.VMEM((8, 1, rows), jnp.float32),
            pltpu.VMEM((128, rows), jnp.float32),
            pltpu.VMEM((64, rows), jnp.float32),
            pltpu.VMEM((rows, 128), jnp.bfloat16),
            dma, dma, dma((len(SENDS),)), dma((8, 4)), dma((8,)), dma((8,)),
            dma((8,)), dma((8,)), dma((8,)), dma((8,)), dma, dma,
        ],
        compiler_params=pltpu.CompilerParams(
            collective_id=0, has_side_effects=True, vmem_limit_bytes=60 << 20
        ),
        name="ladder",
    )(amplitudes, integrals, ij_irrep.reshape(1, rows), cd_irrep.reshape(1, deep))
    return out.T


def solution(mesh):
    in_specs = (P("occ", "vir"), P("vir", "occ"), P("occ"), P("vir"))
    out_specs = P("occ", "vir")
    return jax.shard_map(body, mesh=mesh, in_specs=in_specs, out_specs=out_specs, check_vma=False)
```

time: 290 us -> 119 us (0.41)
  the two profiles are of different devices: /device:TPU:26 before, /device:TPU:66 now
where the time goes in v1:
time: 119 us
  Pallas kernels  117 us (98%)
  local copies, waits for them, and re-layouts  1.67 us (1%)
    pallas_call x1, Pallas kernels, body(): pl.pallas_call(kernel, out_shape=jax.ShapeDtypeStruct((64, rows), jnp.flo...  117 us

profile of v1, /device:TPU:66, one launch (start us, length us, event | category | flops | bytes accessed | tf_op | source)
XLA Modules:
  0.0 118.8 jit_solution(7682369163712976854)
XLA Ops:
  0.0 117.1 %ladder.1 = f32[64,1024]{1,0:T(8,128)} custom-call(bf16[1024,2048]{1,0:T(8,128)(2,1)} %amp_hbm.1, bf16[2048,256]{1,0:T(8,128)(2,1)} %int_hbm.1, s32[1,1024]{1,0:T(1,128)} %bitcast.5, s32[1,2048]{1,0:T(1,128)} %bitcast.4), custom_call_target="tpu_custom_call" | custom-call | tf_op jit(solution)/shard_map/ladder/pallas_call | solution.py:250
  117.1 1.7 %copy.6 = f32[1024,64]{0,1:T(8,128)} copy(f32[1024,64]{0,1:T(8,128)} %bitcast.3) | data formatting | bytes 524288

commit v2 on v1

--- a/solution.py
+++ b/solution.py
@@ -44,6 +44,9 @@
 )
 SENDS = FIRST + tuple(send for event in sorted(FORWARDS) for send in FORWARDS[event])
 LAG = 2
+FOLD = 6
+FOLDED = (2, 4, 5)
+DIRECT = (7, 1, 6, 3)
 TOP = 32767.0
 
 
@@ -60,6 +63,13 @@
     out = jnp.int32(values[-1])
     for at in range(len(values) - 2, -1, -1):
         out = jnp.where(index == at, jnp.int32(values[at]), out)
+    return out
+
+
+def is_in(place, places):
+    out = place == places[0]
+    for other in places[1:]:
+        out = out | (place == other)
     return out
 
 
@@ -136,7 +146,10 @@
     def z_copies(slot):
         target = owner(slot)
         place = (z - target + 8) % 8
-        device = (occ, target * 4 + x_hi * 2 + core)
+        folded = is_in(place, FOLDED)
+        nearer = jnp.where(place == 5, (z + 1) % 8, (z + 7) % 8)
+        place = jnp.where(folded, 8 + slot, place)
+        device = (occ, jnp.where(folded, nearer, target) * 4 + x_hi * 2 + core)
         return (
             pltpu.make_async_remote_copy(
                 src_ref=coded.at[slot], dst_ref=coded_in.at[place],
@@ -157,7 +170,19 @@
     slots = [slot for slot, _ in EVENTS]
     quarters = [quarter for _, quarter in EVENTS]
 
-    @pl.loop(0, len(EVENTS) + LAG)
+    def send(slot, both):
+        most = jnp.maximum(jnp.max(jnp.abs(both), axis=0, keepdims=True), 1e-30)
+        scale[slot] = most * (1.0 / TOP)
+        coded[slot] = jnp.round(both * (TOP / most)).astype(jnp.int32).astype(jnp.int16)
+        for copy in z_copies(slot):
+            copy.start()
+
+    def arrived(place):
+        pltpu.make_async_copy(coded_in.at[place], coded_in.at[place], z_recv.at[place]).wait()
+        pltpu.make_async_copy(scale_in.at[place], scale_in.at[place], s_recv.at[place]).wait()
+        return coded_in[place].astype(jnp.int32).astype(jnp.float32) * scale_in[place]
+
+    @pl.loop(0, len(EVENTS) + LAG + FOLD)
     def _(event):
         @pl.when(event < len(EVENTS))
         def _():
@@ -192,30 +217,39 @@
 
         earlier = jnp.maximum(event - LAG, 0)
 
-        @pl.when((event >= LAG) & (pick(earlier, ends) == 1))
+        @pl.when((event >= LAG) & (event < len(EVENTS) + LAG) & (pick(earlier, ends) == 1))
         def _():
             slot = pick(earlier, slots)
             twin_copy(slot).wait_recv()
             both = turned[slot, core] + twin[slot]
-            here = owner(slot) == z
-
-            @pl.when(here)
+            place = (z - owner(slot) + 8) % 8
+            adds = is_in(place, (1, 3, 6))
+
+            @pl.when(place == 0)
             def _():
                 total[...] = both
 
-            @pl.when(jnp.logical_not(here))
-            def _():
-                most = jnp.maximum(jnp.max(jnp.abs(both), axis=0, keepdims=True), 1e-30)
-                scale[slot] = most * (1.0 / TOP)
-                coded[slot] = jnp.round(both * (TOP / most)).astype(jnp.int32).astype(jnp.int16)
-                for copy in z_copies(slot):
-                    copy.start()
-
-    @pl.loop(1, 8)
-    def _(place):
-        pltpu.make_async_copy(coded_in.at[place], coded_in.at[place], z_recv.at[place]).wait()
-        pltpu.make_async_copy(scale_in.at[place], scale_in.at[place], s_recv.at[place]).wait()
-        total[...] += coded_in[place].astype(jnp.int32).astype(jnp.float32) * scale_in[place]
+            @pl.when(adds)
+            def _():
+                twin[slot] = both
+
+            @pl.when((place != 0) & jnp.logical_not(adds))
+            def _():
+                send(slot, both)
+
+        before = jnp.maximum(event - LAG - FOLD, 0)
+
+        @pl.when((event >= LAG + FOLD) & (pick(before, ends) == 1))
+        def _():
+            slot = pick(before, slots)
+
+            @pl.when(is_in((z - owner(slot) + 8) % 8, (1, 3, 6)))
+            def _():
+                send(slot, twin[slot] + arrived(8 + slot))
+
+    @pl.loop(0, len(DIRECT))
+    def _(at):
+        total[...] += arrived(pick(at, DIRECT))
 
     away = pltpu.make_async_remote_copy(
         src_ref=total.at[pl.ds(pl.multiple_of(64 * (1 - x_hi), 64), 64), :],
@@ -260,13 +294,13 @@
             pltpu.VMEM((8, 128, rows), jnp.float32),
             pltpu.VMEM((8, 128, rows), jnp.int16),
             pltpu.VMEM((8, 1, rows), jnp.float32),
-            pltpu.VMEM((8, 128, rows), jnp.int16),
-            pltpu.VMEM((8, 1, rows), jnp.float32),
+            pltpu.VMEM((16, 128, rows), jnp.int16),
+            pltpu.VMEM((16, 1, rows), jnp.float32),
             pltpu.VMEM((128, rows), jnp.float32),
             pltpu.VMEM((64, rows), jnp.float32),
             pltpu.VMEM((rows, 128), jnp.bfloat16),
             dma, dma, dma((len(SENDS),)), dma((8, 4)), dma((8,)), dma((8,)),
-            dma((8,)), dma((8,)), dma((8,)), dma((8,)), dma, dma,
+            dma((8,)), dma((16,)), dma((8,)), dma((16,)), dma, dma,
         ],
         compiler_params=pltpu.CompilerParams(
             collective_id=0, has_side_effects=True, vmem_limit_bytes=60 << 20

time: 119 us -> 112 us (0.941)
  the two profiles are of different devices: /device:TPU:66 before, /device:TPU:26 now
where the time goes in v2:
time: 112 us
  Pallas kernels  111 us (99%)
  local copies, waits for them, and re-layouts  1.67 us (1%)
    pallas_call x1, Pallas kernels, body(): pl.pallas_call(kernel, out_shape=jax.ShapeDtypeStruct((64, rows), jnp.flo...  111 us

profile of v2, /device:TPU:26, one launch (start us, length us, event | category | flops | bytes accessed | tf_op | source)
XLA Modules:
  0.0 112.2 jit_solution(17937893660962580447)
XLA Ops:
  0.0 110.5 %ladder.1 = f32[64,1024]{1,0:T(8,128)} custom-call(bf16[1024,2048]{1,0:T(8,128)(2,1)} %amp_hbm.1, bf16[2048,256]{1,0:T(8,128)(2,1)} %int_hbm.1, s32[1,1024]{1,0:T(1,128)} %bitcast.5, s32[1,2048]{1,0:T(1,128)} %bitcast.4), custom_call_target="tpu_custom_call" | custom-call | tf_op jit(solution)/shard_map/ladder/pallas_call | solution.py:284
  110.5 1.7 %copy.6 = f32[1024,64]{0,1:T(8,128)} copy(f32[1024,64]{0,1:T(8,128)} %bitcast.3) | data formatting | bytes 524288

commit v3 on v2

--- a/solution.py
+++ b/solution.py
@@ -45,6 +45,7 @@
 SENDS = FIRST + tuple(send for event in sorted(FORWARDS) for send in FORWARDS[event])
 LAG = 2
 FOLD = 6
+PARTS = 4
 FOLDED = (2, 4, 5)
 DIRECT = (7, 1, 6, 3)
 TOP = 32767.0
@@ -83,6 +84,7 @@
     x_lo, y = occ // 4, occ % 4
     z, x_hi, core = vir // 4, (vir // 2) % 2, vir % 2
     depth = int_hbm.shape[0] // 4
+    wide = amp_hbm.shape[0] // PARTS
 
     amp_in = pltpu.make_async_copy(amp_hbm, amp, amp_sem)
     own_in = pltpu.make_async_copy(int_hbm, blocks.at[0], own_sem)
@@ -143,7 +145,7 @@
             device_id_type=MESH,
         )
 
-    def z_copies(slot):
+    def z_copies(slot, part):
         target = owner(slot)
         place = (z - target + 8) % 8
         folded = is_in(place, FOLDED)
@@ -152,13 +154,13 @@
         device = (occ, jnp.where(folded, nearer, target) * 4 + x_hi * 2 + core)
         return (
             pltpu.make_async_remote_copy(
-                src_ref=coded.at[slot], dst_ref=coded_in.at[place],
-                send_sem=z_send.at[slot], recv_sem=z_recv.at[place],
+                src_ref=coded.at[slot, part], dst_ref=coded_in.at[place, part],
+                send_sem=z_send.at[slot, part], recv_sem=z_recv.at[place, part],
                 device_id=device, device_id_type=MESH,
             ),
             pltpu.make_async_remote_copy(
-                src_ref=scale.at[slot], dst_ref=scale_in.at[place],
-                send_sem=s_send.at[slot], recv_sem=s_recv.at[place],
+                src_ref=scale.at[slot, part], dst_ref=scale_in.at[place, part],
+                send_sem=s_send.at[slot, part], recv_sem=s_recv.at[place, part],
                 device_id=device, device_id_type=MESH,
             ),
         )
@@ -170,17 +172,21 @@
     slots = [slot for slot, _ in EVENTS]
     quarters = [quarter for _, quarter in EVENTS]
 
-    def send(slot, both):
+    def send(slot, part, both):
         most = jnp.maximum(jnp.max(jnp.abs(both), axis=0, keepdims=True), 1e-30)
-        scale[slot] = most * (1.0 / TOP)
-        coded[slot] = jnp.round(both * (TOP / most)).astype(jnp.int32).astype(jnp.int16)
-        for copy in z_copies(slot):
+        scale[slot, part] = most * (1.0 / TOP)
+        coded[slot, part] = jnp.round(both * (TOP / most)).astype(jnp.int32).astype(jnp.int16)
+        for copy in z_copies(slot, part):
             copy.start()
 
-    def arrived(place):
-        pltpu.make_async_copy(coded_in.at[place], coded_in.at[place], z_recv.at[place]).wait()
-        pltpu.make_async_copy(scale_in.at[place], scale_in.at[place], s_recv.at[place]).wait()
-        return coded_in[place].astype(jnp.int32).astype(jnp.float32) * scale_in[place]
+    def arrived(place, part):
+        code, step = coded_in.at[place, part], scale_in.at[place, part]
+        pltpu.make_async_copy(code, code, z_recv.at[place, part]).wait()
+        pltpu.make_async_copy(step, step, s_recv.at[place, part]).wait()
+        return coded_in[place, part].astype(jnp.int32).astype(jnp.float32) * scale_in[place, part]
+
+    def columns(part):
+        return slice(part * wide, (part + 1) * wide)
 
     @pl.loop(0, len(EVENTS) + LAG + FOLD)
     def _(event):
@@ -221,21 +227,22 @@
         def _():
             slot = pick(earlier, slots)
             twin_copy(slot).wait_recv()
-            both = turned[slot, core] + twin[slot]
             place = (z - owner(slot) + 8) % 8
             adds = is_in(place, (1, 3, 6))
 
             @pl.when(place == 0)
             def _():
-                total[...] = both
+                for part in range(PARTS):
+                    total[part] = turned[slot, core, :, columns(part)] + twin[slot, :, columns(part)]
 
             @pl.when(adds)
             def _():
-                twin[slot] = both
+                twin[slot] = turned[slot, core] + twin[slot]
 
             @pl.when((place != 0) & jnp.logical_not(adds))
             def _():
-                send(slot, both)
+                for part in range(PARTS):
+                    send(slot, part, turned[slot, core, :, columns(part)] + twin[slot, :, columns(part)])
 
         before = jnp.maximum(event - LAG - FOLD, 0)
 
@@ -245,23 +252,30 @@
 
             @pl.when(is_in((z - owner(slot) + 8) % 8, (1, 3, 6)))
             def _():
-                send(slot, twin[slot] + arrived(8 + slot))
-
-    @pl.loop(0, len(DIRECT))
-    def _(at):
-        total[...] += arrived(pick(at, DIRECT))
-
-    away = pltpu.make_async_remote_copy(
-        src_ref=total.at[pl.ds(pl.multiple_of(64 * (1 - x_hi), 64), 64), :],
-        dst_ref=far,
-        send_sem=far_send, recv_sem=far_recv,
-        device_id=beyond, device_id_type=MESH,
-    )
-    away.start()
-    away.wait_recv()
-    out_ref[...] = total[pl.ds(pl.multiple_of(64 * x_hi, 64), 64), :] + far[...]
-
-    away.wait_send()
+                for part in range(PARTS):
+                    send(slot, part, twin[slot, :, columns(part)] + arrived(8 + slot, part))
+
+    def away(part):
+        return pltpu.make_async_remote_copy(
+            src_ref=total.at[part, pl.ds(pl.multiple_of(64 * (1 - x_hi), 64), 64), :],
+            dst_ref=far.at[part],
+            send_sem=far_send.at[part], recv_sem=far_recv.at[part],
+            device_id=beyond, device_id_type=MESH,
+        )
+
+    for part in range(PARTS):
+        @pl.loop(0, len(DIRECT))
+        def _(at, part=part):
+            total[part] += arrived(pick(at, DIRECT), part)
+
+        away(part).start()
+
+    for part in range(PARTS):
+        away(part).wait_recv()
+        out_ref[:, columns(part)] = total[part, pl.ds(pl.multiple_of(64 * x_hi, 64), 64), :] + far[part]
+
+    for part in range(PARTS):
+        away(part).wait_send()
     for index in range(len(SENDS)):
         piece(index).wait_send()
 
@@ -271,8 +285,9 @@
 
         @pl.when(owner(slot) != z)
         def _():
-            for copy in z_copies(slot):
-                copy.wait_send()
+            for part in range(PARTS):
+                for copy in z_copies(slot, part):
+                    copy.wait_send()
 
 
 def body(amplitudes, integrals, ij_irrep, cd_irrep):
@@ -292,15 +307,15 @@
             pltpu.VMEM((8, rows, wide), jnp.float32),
             pltpu.VMEM((8, 2, 128, rows), jnp.float32),
             pltpu.VMEM((8, 128, rows), jnp.float32),
-            pltpu.VMEM((8, 128, rows), jnp.int16),
-            pltpu.VMEM((8, 1, rows), jnp.float32),
-            pltpu.VMEM((16, 128, rows), jnp.int16),
-            pltpu.VMEM((16, 1, rows), jnp.float32),
-            pltpu.VMEM((128, rows), jnp.float32),
-            pltpu.VMEM((64, rows), jnp.float32),
+            pltpu.VMEM((8, PARTS, 128, rows // PARTS), jnp.int16),
+            pltpu.VMEM((8, PARTS, 1, rows // PARTS), jnp.float32),
+            pltpu.VMEM((16, PARTS, 128, rows // PARTS), jnp.int16),
+            pltpu.VMEM((16, PARTS, 1, rows // PARTS), jnp.float32),
+            pltpu.VMEM((PARTS, 128, rows // PARTS), jnp.float32),
+            pltpu.VMEM((PARTS, 64, rows // PARTS), jnp.float32),
             pltpu.VMEM((rows, 128), jnp.bfloat16),
             dma, dma, dma((len(SENDS),)), dma((8, 4)), dma((8,)), dma((8,)),
-            dma((8,)), dma((16,)), dma((8,)), dma((16,)), dma, dma,
+            dma((8, PARTS)), dma((16, PARTS)), dma((8, PARTS)), dma((16, PARTS)), dma((PARTS,)), dma((PARTS,)),
         ],
         compiler_params=pltpu.CompilerParams(
             collective_id=0, has_side_effects=True, vmem_limit_bytes=60 << 20

time: 112 us -> 109 us (0.973)
  Pallas kernels: 111 us -> 108 us
    pallas_call x1, Pallas kernels: 111 us -> 108 us  [body(): pl.pallas_call(kernel, out_shape=jax.ShapeDtypeStruct((64, rows), jnp.flo...]
where the time goes in v3:
time: 109 us
  Pallas kernels  108 us (99%)
  local copies, waits for them, and re-layouts  1.67 us (2%)
    pallas_call x1, Pallas kernels, body(): pl.pallas_call(kernel, out_shape=jax.ShapeDtypeStruct((64, rows), jnp.flo...  108 us

profile of v3, /device:TPU:26, one launch (start us, length us, event | category | flops | bytes accessed | tf_op | source)
XLA Modules:
  0.0 109.2 jit_solution(17084053490748203674)
XLA Ops:
  0.0 107.5 %ladder.1 = f32[64,1024]{1,0:T(8,128)} custom-call(bf16[1024,2048]{1,0:T(8,128)(2,1)} %amp_hbm.1, bf16[2048,256]{1,0:T(8,128)(2,1)} %int_hbm.1, s32[1,1024]{1,0:T(1,128)} %bitcast.5, s32[1,2048]{1,0:T(1,128)} %bitcast.4), custom_call_target="tpu_custom_call" | custom-call | tf_op jit(solution)/shard_map/ladder/pallas_call | solution.py:299
  107.5 1.7 %copy.6 = f32[1024,64]{0,1:T(8,128)} copy(f32[1024,64]{0,1:T(8,128)} %bitcast.3) | data formatting | bytes 524288

commit v4 on v3

--- a/solution.py
+++ b/solution.py
@@ -43,8 +43,8 @@
     ("up", 0, 3), ("down", 0, 2), ("across", 0, 3),
 )
 SENDS = FIRST + tuple(send for event in sorted(FORWARDS) for send in FORWARDS[event])
-LAG = 2
-FOLD = 6
+LAG = 1
+FOLD = 8
 PARTS = 4
 FOLDED = (2, 4, 5)
 DIRECT = (7, 1, 6, 3)
@@ -135,12 +135,15 @@
         step = pick(slot, [WHERE[at][1] for at in range(8)])
         return ((x_lo + other) % 2) * 4 + (y + step) % 4
 
-    def twin_copy(slot):
+    def columns(part):
+        return slice(part * wide, (part + 1) * wide)
+
+    def twin_copy(slot, part):
         return pltpu.make_async_remote_copy(
-            src_ref=turned.at[slot, 1 - core],
-            dst_ref=twin.at[slot],
-            send_sem=twin_send.at[slot],
-            recv_sem=twin_recv.at[slot],
+            src_ref=turned.at[slot, 1 - core, :, columns(part)],
+            dst_ref=twin.at[slot, :, columns(part)],
+            send_sem=twin_send.at[slot, part],
+            recv_sem=twin_recv.at[slot, part],
             device_id=sibling,
             device_id_type=MESH,
         )
@@ -185,8 +188,9 @@
         pltpu.make_async_copy(step, step, s_recv.at[place, part]).wait()
         return coded_in[place, part].astype(jnp.int32).astype(jnp.float32) * scale_in[place, part]
 
-    def columns(part):
-        return slice(part * wide, (part + 1) * wide)
+    def both(slot, part):
+        twin_copy(slot, part).wait_recv()
+        return turned[slot, core, :, columns(part)] + twin[slot, :, columns(part)]
 
     @pl.loop(0, len(EVENTS) + LAG + FOLD)
     def _(event):
@@ -215,34 +219,35 @@
 
             @pl.when(pick(event, ends) == 1)
             def _():
-                block = acc[slot].T
-                for half in range(2):
-                    turned[slot, half, 0:64, :] = block[64 * half:64 * half + 64]
-                    turned[slot, half, 64:128, :] = block[128 + 64 * half:192 + 64 * half]
-                twin_copy(slot).start()
+                for part in range(PARTS):
+                    block = acc[slot, columns(part), :].T
+                    for half in range(2):
+                        turned[slot, half, 0:64, columns(part)] = block[64 * half:64 * half + 64]
+                        turned[slot, half, 64:128, columns(part)] = block[128 + 64 * half:192 + 64 * half]
+                    twin_copy(slot, part).start()
 
         earlier = jnp.maximum(event - LAG, 0)
 
         @pl.when((event >= LAG) & (event < len(EVENTS) + LAG) & (pick(earlier, ends) == 1))
         def _():
             slot = pick(earlier, slots)
-            twin_copy(slot).wait_recv()
             place = (z - owner(slot) + 8) % 8
             adds = is_in(place, (1, 3, 6))
 
             @pl.when(place == 0)
             def _():
                 for part in range(PARTS):
-                    total[part] = turned[slot, core, :, columns(part)] + twin[slot, :, columns(part)]
+                    total[part] = both(slot, part)
 
             @pl.when(adds)
             def _():
-                twin[slot] = turned[slot, core] + twin[slot]
+                for part in range(PARTS):
+                    twin[slot, :, columns(part)] = both(slot, part)
 
             @pl.when((place != 0) & jnp.logical_not(adds))
             def _():
                 for part in range(PARTS):
-                    send(slot, part, turned[slot, core, :, columns(part)] + twin[slot, :, columns(part)])
+                    send(slot, part, both(slot, part))
 
         before = jnp.maximum(event - LAG - FOLD, 0)
 
@@ -281,7 +286,8 @@
 
     @pl.loop(0, 8)
     def _(slot):
-        twin_copy(slot).wait_send()
+        for part in range(PARTS):
+            twin_copy(slot, part).wait_send()
 
         @pl.when(owner(slot) != z)
         def _():
@@ -314,7 +320,7 @@
             pltpu.VMEM((PARTS, 128, rows // PARTS), jnp.float32),
             pltpu.VMEM((PARTS, 64, rows // PARTS), jnp.float32),
             pltpu.VMEM((rows, 128), jnp.bfloat16),
-            dma, dma, dma((len(SENDS),)), dma((8, 4)), dma((8,)), dma((8,)),
+            dma, dma, dma((len(SENDS),)), dma((8, 4)), dma((8, PARTS)), dma((8, PARTS)),
             dma((8, PARTS)), dma((16, PARTS)), dma((8, PARTS)), dma((16, PARTS)), dma((PARTS,)), dma((PARTS,)),
         ],
         compiler_params=pltpu.CompilerParams(

time: 109 us -> 109 us (level)
  no operation moved by 1% of the time
where the time goes in v4:
time: 109 us
  Pallas kernels  107 us (98%)
  local copies, waits for them, and re-layouts  1.67 us (2%)
    pallas_call x1, Pallas kernels, body(): pl.pallas_call(kernel, out_shape=jax.ShapeDtypeStruct((64, rows), jnp.flo...  107 us

profile of v4, /device:TPU:26, one launch (start us, length us, event | category | flops | bytes accessed | tf_op | source)
XLA Modules:
  0.0 108.9 jit_solution(3403199457820320310)
XLA Ops:
  0.0 107.2 %ladder.1 = f32[64,1024]{1,0:T(8,128)} custom-call(bf16[1024,2048]{1,0:T(8,128)(2,1)} %amp_hbm.1, bf16[2048,256]{1,0:T(8,128)(2,1)} %int_hbm.1, s32[1,1024]{1,0:T(1,128)} %bitcast.5, s32[1,2048]{1,0:T(1,128)} %bitcast.4), custom_call_target="tpu_custom_call" | custom-call | tf_op jit(solution)/shard_map/ladder/pallas_call | solution.py:305
  107.2 1.7 %copy.6 = f32[1024,64]{0,1:T(8,128)} copy(f32[1024,64]{0,1:T(8,128)} %bitcast.3) | data formatting | bytes 524288
